TPU v7x, 32 devices: a whole 2x2x4 slice. The times are simulated.
32 devices in a mesh: tiles: 2 (over x), space: 8 (over z, y), chan: 2 (over core).
Axes of the slice: x: 2, y: 2, z: 4, core: 2. Of those that a mesh axis runs over, the one named last changes fastest.
Arguments:
- volume: bfloat16 [32, 64, 32, 256], P(None, 'space', 'tiles', 'chan'), parts along dimension 2, may hold values from -6 to 6
- weight_one: bfloat16 [3, 3, 3, 256, 256], replicated, may hold values from -0.078125 to 0.078125
- bias_one: float32 [256], replicated, may hold values from -3 to 3
- weight_two: bfloat16 [3, 3, 3, 256, 256], replicated, may hold values from -0.078125 to 0.078125
- bias_two: float32 [256], replicated, may hold values from -3 to 3
Outputs:
- features: bfloat16 [32, 64, 32, 256], P('space', None, 'tiles', 'chan'), parts along dimension 2
There are 2 independent parts, one for each index of `tiles`. A program takes and returns all parts, laid end to end along the dimension named above; an argument that names none is the same for every part. Nothing has to cross between parts.
All inputs are finite; a program needn't handle non-finite values.
Results may differ from a plain program's by a relative error of at most 0.0044.
Values may be sent and summed in bfloat16 or wider, within the bound.
A program may use at most 128 MiB of HBM per device.

v0:
```python
import jax
import jax.numpy as jnp
from jax import lax
from jax.sharding import PartitionSpec as P


def padded(x, sides, width):
    for axis, dim in sides:
        devices, length = (lax.axis_size(axis), x.shape[dim])
        up = [(i, (i + 1) % devices) for i in range(devices - 1)]
        down = [(j, i) for i, j in up]
        last = lax.slice_in_dim(x, length - width, length, axis=dim)
        first = lax.slice_in_dim(x, 0, width, axis=dim)
        before = lax.ppermute(last, axis, up)
        after = lax.ppermute(first, axis, down)
        x = jnp.concatenate([before, x, after], axis=dim)
    return x


def convolve(field, kernel):
    return lax.conv_general_dilated(
        field[None],
        kernel,
        (1, 1, 1),
        ((0, 0), (1, 1), (1, 1)),
        dimension_numbers=("NDHWC", "DHWIO", "NDHWC"),
        preferred_element_type=jnp.float32,
    )[0]


def pad_layer(field):
    return padded(field, (("space", 0),), 1)


def body(volume, weight_one, bias_one, weight_two, bias_two):
    slab_data = lax.all_to_all(volume, "space", split_axis=0, concat_axis=1, tiled=True)
    share = slab_data.shape[3]
    offset = lax.axis_index("chan") * share

    def layer(field, kernel, bias):
        part_kernel = lax.dynamic_slice_in_dim(kernel, offset, share, 3)
        summed = lax.psum_scatter(
            convolve(field, part_kernel), "chan", scatter_dimension=3, tiled=True
        )
        return summed + lax.dynamic_slice_in_dim(bias, offset, share, 0)

    hidden = jnp.maximum(layer(pad_layer(slab_data), weight_one, bias_one), 0.0).astype(
        jnp.bfloat16
    )
    result = layer(pad_layer(hidden), weight_two, bias_two)
    return jnp.maximum(result, 0.0).astype(jnp.bfloat16)


def solution(mesh):
    return jax.shard_map(
        body,
        mesh=mesh,
        in_specs=(P(None, "space", "tiles", "chan"), P(), P(), P(), P()),
        out_specs=P("space", None, "tiles", "chan"),
        check_vma=False,
    )
```

profile of v0, /device:TPU:0, one launch (start us, length us, event | category | flops | bytes accessed | tf_op | source)
XLA Modules:
  0.0 152.2 jit_solution(18392344283605213715)
XLA Ops:
  6.5 33.3 %all_to_all.18 = bf16[32,8,16,128]{3,2,1,0:T(8,128)(2,1)S(1)} all-to-all(bf16[32,8,16,128]{3,2,1,0:T(8,128)(2,1)} %param.5), channel_id=1, replica_groups=mesh['tiles'=2,'space'=8,'chan'=2] {'space'}, dimensions={0} | all-to-all | bytes 2097152 | tf_op jit(solution)/shard_map/all_to_all | solution.py:36
  39.9 1.0 copy-done.2
  40.8 0.8 fusion.33
  41.7 4.1 %collective-permute-start = (bf16[1,64,16,128]{3,2,1,0:T(8,128)(2,1)}, bf16[1,64,16,128]{3,2,1,0:T(8,128)(2,1)}, u32[]{:S(2)}, u32[]{:S(2)}) collective-permute-start(bf16[1,64,16,128]{3,2,1,0:T(8,128)(2,1)} %bitcast.2), channel_id=1, source_target_pairs={{0,2},{2,4},{4,6},{6,8},{8,10},{10,12},{12,14},{1,3},{3,5},{5,7},{... | collective-permute-start | bytes 786440 | tf_op jit(solution)/shard_map/ppermute | solution.py:14
  45.7 1.3 collective-permute-start.1
  47.0 1.4 copy.14
  48.4 6.9 %collective-permute-done = bf16[1,64,16,128]{3,2,1,0:T(8,128)(2,1)} collective-permute-done((bf16[1,64,16,128]{3,2,1,0:T(8,128)(2,1)}, bf16[1,64,16,128]{3,2,1,0:T(8,128)(2,1)}, u32[]{:S(2)}, u32[]{:S(2)}) %collective-permute-start) | collective-permute-done | bytes 262176 | tf_op jit(solution)/shard_map/ppermute | solution.py:14
  55.4 1.2 maximum_bitcast_fusion
  56.6 0.4 copy.23
  57.0 0.4 pad.clone
  57.4 1.5 %copy.17 = bf16[6,64,1,8,3,128]{5,3,4,1,0,2:T(8,128)(2,1)S(1)} copy(bf16[6,64,1,8,3,128]{5,1,4,3,0,2:T(8,128)(2,1)S(1)} %bitcast.31) | data formatting | bytes 4718592 | tf_op jit(solution)/shard_map/conv_general_dilated | solution.py:21
  58.9 0.4 slice.30
  59.4 0.2 copy-done.6
  59.6 13.5 %broadcast_select_fusion.1 = f32[4,64,8,3,256]{4,2,3,1,0:T(8,128)S(1)} fusion(pred[8,3]{0,1:T(4,128)(4,1)S(1)} %copy-done.6, bf16[6,64,1,7,2,128]{5,3,4,1,0,2:T(8,128)(2,1)S(1)} %slice.30, bf16[6,64,1,8,3,128]{5,3,4,1,0,2:T(8,128)(2,1)S(1)} %copy.17, bf16[3,3,3,256,256]{4,3,2,1,0:T(8,128)(2,1)S(1)} %copy-done, s32[]{:T(128)S(6)} %select_n.2), kind=kOutput, calls=%fused_computation.18 | convolution fusion | flops 10771759104 | bytes 11993604 | tf_op jit(solution)/shard_map/conv_general_dilated | solution.py:21
  73.0 1.9 %copy.18 = f32[4,64,8,3,256]{4,1,3,2,0:T(8,128)S(1)} copy(f32[4,64,8,3,256]{4,2,3,1,0:T(8,128)S(1)} %broadcast_select_fusion.1) | data formatting | bytes 12582912 | tf_op jit(solution)/shard_map/conv_general_dilated | solution.py:21
  75.0 2.4 %slice_bitcast_fusion.1 = f32[4,64,16,256]{3,1,2,0:T(8,128)} fusion(f32[4,64,1,24,256]{4,1,3,0,2:T(8,128)S(1)} %bitcast.28), kind=kLoop, calls=%fused_computation.4 | loop fusion | bytes 8388608 | tf_op jit(solution)/shard_map/squeeze | solution.py:21
  77.5 0.6 copy-done.4
  78.2 11.9 %reduce-scatter.3.cloned.1.call-done = f32[4,64,16,128]{3,1,2,0:T(8,128)} async-done(((f32[4,64,16,256]{3,1,2,0:T(8,128)}), f32[4,64,16,128]{3,1,2,0:T(8,128)}) %reduce-scatter.3.cloned.1.call-update) | async-done | bytes 2097168 | tf_op jit(solution)/shard_map/reduce_scatter | solution.py:42
  90.1 1.9 %maximum_convert_fusion.1 = bf16[4,64,16,128]{3,1,2,0:T(8,128)(2,1)S(1)} fusion(f32[4,64,16,128]{3,1,2,0:T(8,128)} %reduce-scatter.3.cloned.1.call-done, f32[128]{0:T(128)S(1)} %dynamic_slice.13), kind=kLoop, calls=%fused_computation.20 | loop fusion | flops 1572864 | bytes 3146240 | tf_op jit(solution)/shard_map/convert_element_type | solution.py:47
  92.0 3.8 %collective-permute-start.2 = (bf16[1,64,16,128]{3,1,2,0:T(8,128)(2,1)S(1)}, bf16[1,64,16,128]{3,1,2,0:T(8,128)(2,1)S(1)}, u32[]{:S(2)}, u32[]{:S(2)}) collective-permute-start(bf16[1,64,16,128]{3,1,2,0:T(8,128)(2,1)S(1)} %get-tuple-element.5), channel_id=1, source_target_pairs={{0,2},{2,4},{4,6},{6,8},{8,10},{10,12},{12,14},{1,3},{3,5},{5,7},{... | collective-permute-start | bytes 786440 | tf_op jit(solution)/shard_map/ppermute | solution.py:14
  95.8 1.5 collective-permute-start.3
  97.2 10.0 %collective-permute-done.2 = bf16[1,64,16,128]{3,1,2,0:T(8,128)(2,1)S(1)} collective-permute-done((bf16[1,64,16,128]{3,1,2,0:T(8,128)(2,1)S(1)}, bf16[1,64,16,128]{3,1,2,0:T(8,128)(2,1)S(1)}, u32[]{:S(2)}, u32[]{:S(2)}) %collective-permute-start.2) | collective-permute-done | bytes 262176 | tf_op jit(solution)/shard_map/ppermute | solution.py:14
  107.5 0.4 pad.2
  107.9 1.5 %copy.20 = bf16[6,64,1,8,3,128]{5,3,4,1,0,2:T(8,128)(2,1)S(1)} copy(bf16[6,64,1,8,3,128]{5,1,4,3,0,2:T(8,128)(2,1)S(1)} %bitcast.30) | data formatting | bytes 4718592 | tf_op jit(solution)/shard_map/conv_general_dilated | solution.py:21
  109.4 0.4 slice.34
  109.9 13.5 %broadcast_select_fusion = f32[4,64,8,3,256]{4,2,3,1,0:T(8,128)S(1)} fusion(pred[8,3]{0,1:T(4,128)(4,1)S(1)} %copy-done.6, bf16[6,64,1,7,2,128]{5,3,4,1,0,2:T(8,128)(2,1)S(1)} %slice.34, bf16[6,64,1,8,3,128]{5,3,4,1,0,2:T(8,128)(2,1)S(1)} %copy.20, bf16[3,3,3,256,256]{4,3,2,1,0:T(8,128)(2,1)S(1)} %copy-done.3, s32[]{:T(128)S(6)} %select_n.2), kind=kOutput, calls=%fused_computation.17 | convolution fusion | flops 10771759104 | bytes 11993604 | tf_op jit(solution)/shard_map/conv_general_dilated | solution.py:21
  123.3 1.9 %copy.21 = f32[4,64,8,3,256]{4,1,3,2,0:T(8,128)S(1)} copy(f32[4,64,8,3,256]{4,2,3,1,0:T(8,128)S(1)} %broadcast_select_fusion) | data formatting | bytes 12582912 | tf_op jit(solution)/shard_map/conv_general_dilated | solution.py:21
  125.3 2.4 %slice_bitcast_fusion = f32[4,64,16,256]{3,1,2,0:T(8,128)} fusion(f32[4,64,1,24,256]{4,1,3,0,2:T(8,128)S(1)} %bitcast.29), kind=kLoop, calls=%fused_computation.3 | loop fusion | bytes 8388608 | tf_op jit(solution)/shard_map/squeeze | solution.py:21
  127.8 0.7 copy-done.5
  128.5 13.4 %reduce-scatter.5.cloned.1.call-done = f32[4,64,16,128]{3,1,2,0:T(8,128)} async-done(((f32[4,64,16,256]{3,1,2,0:T(8,128)}), f32[4,64,16,128]{3,1,2,0:T(8,128)}) %reduce-scatter.5.cloned.1.call-update) | async-done | bytes 2097168 | tf_op jit(solution)/shard_map/reduce_scatter | solution.py:42
  141.8 1.9 %maximum_convert_fusion = bf16[4,64,16,128]{3,1,2,0:T(8,128)(2,1)S(1)} fusion(f32[4,64,16,128]{3,1,2,0:T(8,128)} %reduce-scatter.5.cloned.1.call-done, f32[128]{0:T(128)S(1)} %dynamic_slice.15), kind=kLoop, calls=%fused_computation.19 | loop fusion | flops 1572864 | bytes 3146240 | tf_op jit(solution)/shard_map/convert_element_type | solution.py:51
  143.7 1.7 %copy.22 = bf16[4,64,16,128]{3,2,1,0:T(8,128)(2,1)} copy(bf16[4,64,16,128]{3,1,2,0:T(8,128)(2,1)S(1)} %maximum_convert_fusion) | data formatting | bytes 2097152 | tf_op jit(solution)/shard_map/convert_element_type | solution.py:51
  (20 shorter events, 0.5 us)
Async XLA Ops:
  6.5 52.8 %copy-start = (bf16[3,3,3,256,256]{4,3,2,1,0:T(8,128)(2,1)S(1)}, bf16[3,3,3,256,256]{4,3,2,1,0:T(8,128)(2,1)}, u32[]{:S(2)}) copy-start(bf16[3,3,3,256,256]{4,3,2,1,0:T(8,128)(2,1)} %param.6) | copy-start | bytes 10616836
  6.5 83.5 %reduce-scatter.3.cloned.1.call-start = ((), (), s32[]{:S(2)}) async-start(), calls=%async_computation.3 | async-start | bytes 6291456 | tf_op jit(solution)/shard_map/reduce_scatter | solution.py:42
  39.9 1.0 copy-start.2
  41.7 13.7 %collective-permute-start = (bf16[1,64,16,128]{3,2,1,0:T(8,128)(2,1)}, bf16[1,64,16,128]{3,2,1,0:T(8,128)(2,1)}, u32[]{:S(2)}, u32[]{:S(2)}) collective-permute-start(bf16[1,64,16,128]{3,2,1,0:T(8,128)(2,1)} %bitcast.2), channel_id=1, source_target_pairs={{0,2},{2,4},{4,6},{6,8},{8,10},{10,12},{12,14},{1,3},{3,5},{5,7},{... | collective-permute-start | bytes 786440 | tf_op jit(solution)/shard_map/ppermute | solution.py:14
  45.7 9.6 %collective-permute-start.1 = (bf16[1,64,16,128]{3,2,1,0:T(8,128)(2,1)}, bf16[1,64,16,128]{3,2,1,0:T(8,128)(2,1)}, u32[]{:S(2)}, u32[]{:S(2)}) collective-permute-start(bf16[1,64,16,128]{3,2,1,0:T(8,128)(2,1)} %bitcast.5), channel_id=1, source_target_pairs={{2,0},{4,2},{6,4},{8,6},{10,8},{12,10},{14,12},{3,1},{5,3},{7,5},{... | collective-permute-start | bytes 786440 | tf_op jit(solution)/shard_map/ppermute | solution.py:15
  58.9 0.7 copy-start.6
  77.4 0.7 copy-start.4
  77.4 64.4 %reduce-scatter.5.cloned.1.call-start = ((), (), s32[]{:S(2)}) async-start(), calls=%async_computation.4 | async-start | bytes 6291456 | tf_op jit(solution)/shard_map/reduce_scatter | solution.py:42
  92.0 15.3 %collective-permute-start.2 = (bf16[1,64,16,128]{3,1,2,0:T(8,128)(2,1)S(1)}, bf16[1,64,16,128]{3,1,2,0:T(8,128)(2,1)S(1)}, u32[]{:S(2)}, u32[]{:S(2)}) collective-permute-start(bf16[1,64,16,128]{3,1,2,0:T(8,128)(2,1)S(1)} %get-tuple-element.5), channel_id=1, source_target_pairs={{0,2},{2,4},{4,6},{6,8},{8,10},{10,12},{12,14},{1,3},{3,5},{5,7},{... | collective-permute-start | bytes 786440 | tf_op jit(solution)/shard_map/ppermute | solution.py:14
  95.8 11.5 %collective-permute-start.3 = (bf16[1,64,16,128]{3,1,2,0:T(8,128)(2,1)S(1)}, bf16[1,64,16,128]{3,1,2,0:T(8,128)(2,1)S(1)}, u32[]{:S(2)}, u32[]{:S(2)}) collective-permute-start(bf16[1,64,16,128]{3,1,2,0:T(8,128)(2,1)S(1)} %get-tuple-element.6), channel_id=1, source_target_pairs={{2,0},{4,2},{6,4},{8,6},{10,8},{12,10},{14,12},{3,1},{5,3},{7,5},{... | collective-permute-start | bytes 786440 | tf_op jit(solution)/shard_map/ppermute | solution.py:15
  107.8 2.0 %copy-start.3 = (bf16[3,3,3,256,256]{4,3,2,1,0:T(8,128)(2,1)S(1)}, bf16[3,3,3,256,256]{4,3,2,1,0:T(8,128)(2,1)}, u32[]{:S(2)}) copy-start(bf16[3,3,3,256,256]{4,3,2,1,0:T(8,128)(2,1)} %param.8) | copy-start | bytes 10616836
  127.7 0.7 copy-start.5
  128.4 17.0 %copy-start.1 = (bf16[3,3,3,256,256]{4,3,2,1,0:T(8,128)(2,1)S(1)}, bf16[3,3,3,256,256]{4,3,2,1,0:T(8,128)(2,1)}, u32[]{:S(2)}) copy-start(bf16[3,3,3,256,256]{4,3,2,1,0:T(8,128)(2,1)} %param.6) | copy-start | bytes 10616836
Sparse Core Ops, SparseCore 0:
  77.6 12.4 reduce-scatter.2
  127.9 13.9 reduce-scatter.4
where the time goes:
time: 153 us; the launch traced here: 152 us
  waiting for transfers between devices  42.2 us (28%)
  blocking collectives  33.3 us (22%)
  matrix products  26.9 us (18%)
  local copies, waits for them, and re-layouts  20.4 us (13%)
  between operations  13.6 us (9%)
  starting transfers between devices  10.6 us (7%)
  other arithmetic  5.18 us (3%)
    all_to_all x1, blocking collectives, body(): lax.all_to_all(volume, 'space', split_axis=0, concat_axis=1, tiled=True)  33.3 us
    conv_general_dilated x2, matrix products, convolve(): lax.conv_general_dilated(field[None], kernel, (1, 1, 1), ((0, 0), (1, 1),...  26.9 us
    reduce_scatter x2, waiting for transfers between devices, layer(): lax.psum_scatter(convolve(field, part_kernel), 'chan', scatter_dimension=...  25.3 us
    ppermute x2, waiting for transfers between devices, padded(): before = lax.ppermute(last, axis, up)  17 us
    ppermute x2, starting transfers between devices, padded(): before = lax.ppermute(last, axis, up)  7.83 us
    conv_general_dilated x6, local copies, waits for them, and re-layouts, convolve(): lax.conv_general_dilated(field[None], kernel, (1, 1, 1), ((0, 0), (1, 1),...  7.73 us
    squeeze x2, local copies, waits for them, and re-layouts, convolve(): lax.conv_general_dilated(field[None], kernel, (1, 1, 1), ((0, 0), (1, 1),...  4.89 us
  transfers between devices with their start and end apart: 6, of which 4 were waited for; matrix products, arithmetic and copies ran while one was open for 1% of the time, Pallas kernels for 0%

commit v1 on v0

--- a/solution.py
+++ b/solution.py
@@ -2,6 +2,18 @@
 import jax.numpy as jnp
 from jax import lax
 from jax.sharding import PartitionSpec as P
+
+
+def cut_along(value, dim, size):
+    shape = value.shape
+    blocks = value.reshape(*shape[:dim], size, shape[dim] // size, *shape[dim + 1 :])
+    return jnp.moveaxis(blocks, dim, 0)
+
+
+def joined_along(blocks, dim):
+    blocks = jnp.moveaxis(blocks, 0, dim)
+    lengths = blocks.shape
+    return blocks.reshape(*lengths[:dim], lengths[dim] * lengths[dim + 1], *lengths[dim + 2 :])
 
 
 def padded(x, sides, width):
@@ -33,7 +45,14 @@
 
 
 def body(volume, weight_one, bias_one, weight_two, bias_two):
-    slab_data = lax.all_to_all(volume, "space", split_axis=0, concat_axis=1, tiled=True)
+    length_2, index = (lax.axis_size("space"), lax.axis_index("space"))
+    tiles = cut_along(volume, 0, length_2)
+    outs = [tiles[index]]
+    for step in range(1, length_2):
+        sent = tiles[index ^ step]
+        outs.append(lax.ppermute(sent, "space", [(i_2, i_2 ^ step) for i_2 in range(length_2)]))
+    tiles = jnp.stack(outs)[index ^ jnp.arange(length_2)]
+    slab_data = joined_along(tiles, 1)
     share = slab_data.shape[3]
     offset = lax.axis_index("chan") * share
 

time: 153 us -> 157 us (1.026)
  blocking collectives: 33.3 us -> 0 us
  waiting for transfers between devices: 42.2 us -> 56.8 us
  starting transfers between devices: 10.6 us -> 23.8 us
  local copies, waits for them, and re-layouts: 20.4 us -> 30.4 us
    all_to_all x1 -> x0, blocking collectives: 33.3 us -> none  [body(): lax.all_to_all(volume, 'space', split_axis=0, concat_axis=1, tiled=True)]
    ppermute x0 -> x7, starting transfers between devices: none -> 13.1 us  [body(): lax.ppermute(sent, 'space', [(i_2, i_2 ^ step) for i_2 in range(length_2)])]
    ppermute x2, waiting for transfers between devices: 0.01 us -> 12.1 us  [padded(): after = lax.ppermute(first, axis, down)]
    ppermute x0 -> x7, waiting for transfers between devices: none -> 11.2 us  [body(): lax.ppermute(sent, 'space', [(i_2, i_2 ^ step) for i_2 in range(length_2)])]
    ppermute x2, waiting for transfers between devices: 17 us -> 6.52 us  [padded(): before = lax.ppermute(last, axis, up)]
    unnamed x15 -> x19, local copies, waits for them, and re-layouts: 2.91 us -> 5.93 us
    gather x0 -> x1, local copies, waits for them, and re-layouts: none -> 2.89 us  [body(): tiles = jnp.stack(outs)[index ^ jnp.arange(length_2)]]
    squeeze x0 -> x1, local copies, waits for them, and re-layouts: none -> 2.4 us  [body(): sent = tiles[index ^ step]]
  transfers between devices with their start and end apart: 6 -> 13, of which waited for: 4 -> 8; matrix products, arithmetic and copies ran while one was open for 1% -> 4% of each run, Pallas kernels for 0% -> 0%
where the time goes in v1:
time: 157 us
  waiting for transfers between devices  56.8 us (36%)
  local copies, waits for them, and re-layouts  30.4 us (19%)
  matrix products  26.9 us (17%)
  starting transfers between devices  23.8 us (15%)
  between operations  13.6 us (9%)
  other arithmetic  5.19 us (3%)
    reduce_scatter x2, waiting for transfers between devices, layer(): lax.psum_scatter(convolve(field, part_kernel), 'chan', scatter_dimension=...  27.1 us
    conv_general_dilated x2, matrix products, convolve(): lax.conv_general_dilated(field[None], kernel, (1, 1, 1), ((0, 0), (1, 1),...  26.9 us
    ppermute x7, starting transfers between devices, body(): lax.ppermute(sent, 'space', [(i_2, i_2 ^ step) for i_2 in range(length_2)])  13.1 us
    ppermute x2, waiting for transfers between devices, padded(): after = lax.ppermute(first, axis, down)  12.1 us
    ppermute x7, waiting for transfers between devices, body(): lax.ppermute(sent, 'space', [(i_2, i_2 ^ step) for i_2 in range(length_2)])  11.2 us
    ppermute x2, starting transfers between devices, padded(): before = lax.ppermute(last, axis, up)  8.06 us
    conv_general_dilated x6, local copies, waits for them, and re-layouts, convolve(): lax.conv_general_dilated(field[None], kernel, (1, 1, 1), ((0, 0), (1, 1),...  7.73 us
    ppermute x2, waiting for transfers between devices, padded(): before = lax.ppermute(last, axis, up)  6.52 us
  transfers between devices with their start and end apart: 13, of which 8 were waited for; matrix products, arithmetic and copies ran while one was open for 4% of the time, Pallas kernels for 0%

profile of v1, /device:TPU:0, one launch (start us, length us, event | category | flops | bytes accessed | tf_op | source)
XLA Modules:
  0.0 156.8 jit_solution(14129470438218797391)
XLA Ops:
  6.5 2.4 %dynamic-slice_bitcast_fusion = (bf16[4,8,16,128]{3,2,1,0:T(8,128)(2,1)S(1)}, bf16[4,8,16,128]{3,2,1,0:T(8,128)(2,1)S(1)}, bf16[4,8,16,128]{3,2,1,0:T(8,128)(2,1...) fusion(bf16[8,4,8,16,128]{4,3,2,1,0:T(8,128)(2,1)} %bitcast.64,, ...), kind=kLoop, calls=%fused_computation.35 | loop fusion | bytes 2097184 | tf_op jit(solution)/shard_map/squeeze | solution.py:52
  8.9 3.0 %collective-permute-start = (bf16[4,8,16,128]{3,2,1,0:T(8,128)(2,1)S(1)}, bf16[4,8,16,128]{3,2,1,0:T(8,128)(2,1)S(1)}, u32[]{:S(2)}, u32[]{:S(2)}) collective-permute-start(bf16[4,8,16,128]{3,2,1,0:T(8,128)(2,1)S(1)} %get-tuple-element.15), channel_id=1, source_target_pairs={{0,2},{2,0},{4,6},{6,4},{8,10},{10,8},{12,14},{14,12},{1,3},{3,1},... | collective-permute-start | bytes 393224 | tf_op jit(solution)/shard_map/ppermute | solution.py:53
  11.9 1.6 %collective-permute-start.1 = (bf16[4,8,16,128]{3,2,1,0:T(8,128)(2,1)S(1)}, bf16[4,8,16,128]{3,2,1,0:T(8,128)(2,1)S(1)}, u32[]{:S(2)}, u32[]{:S(2)}) collective-permute-start(bf16[4,8,16,128]{3,2,1,0:T(8,128)(2,1)S(1)} %get-tuple-element.14), channel_id=1, source_target_pairs={{0,4},{2,6},{4,0},{6,2},{8,12},{10,14},{12,8},{14,10},{1,5},{3,7},... | collective-permute-start | bytes 393224 | tf_op jit(solution)/shard_map/ppermute | solution.py:53
  13.5 3.0 %collective-permute-start.3 = (bf16[4,8,16,128]{3,2,1,0:T(8,128)(2,1)S(1)}, bf16[4,8,16,128]{3,2,1,0:T(8,128)(2,1)S(1)}, u32[]{:S(2)}, u32[]{:S(2)}) collective-permute-start(bf16[4,8,16,128]{3,2,1,0:T(8,128)(2,1)S(1)} %get-tuple-element.12), channel_id=1, source_target_pairs={{0,8},{2,10},{4,12},{6,14},{8,0},{10,2},{12,4},{14,6},{1,9},{3,11}... | collective-permute-start | bytes 393224 | tf_op jit(solution)/shard_map/ppermute | solution.py:53
  16.5 1.3 collective-permute-start.4
  17.8 3.7 %collective-permute-start.5 = (bf16[4,8,16,128]{3,2,1,0:T(8,128)(2,1)S(1)}, bf16[4,8,16,128]{3,2,1,0:T(8,128)(2,1)S(1)}, u32[]{:S(2)}, u32[]{:S(2)}) collective-permute-start(bf16[4,8,16,128]{3,2,1,0:T(8,128)(2,1)S(1)} %get-tuple-element.10), channel_id=1, source_target_pairs={{0,12},{2,14},{4,8},{6,10},{8,4},{10,6},{12,0},{14,2},{1,13},{3,15... | collective-permute-start | bytes 393224 | tf_op jit(solution)/shard_map/ppermute | solution.py:53
  25.3 10.6 %collective-permute-done.4 = bf16[4,8,16,128]{3,2,1,0:T(8,128)(2,1)S(1)} collective-permute-done((bf16[4,8,16,128]{3,2,1,0:T(8,128)(2,1)S(1)}, bf16[4,8,16,128]{3,2,1,0:T(8,128)(2,1)S(1)}, u32[]{:S(2)}, u32[]{:S(2)}) %collective-permute-start.4) | collective-permute-done | bytes 131104 | tf_op jit(solution)/shard_map/ppermute | solution.py:53
  37.9 2.9 %gather_fusion = bf16[8,4,8,16,128]{4,3,2,1,0:T(8,128)(2,1)} fusion(bf16[8,4,8,16,128]{4,3,2,1,0:T(8,128)(2,1)} %bitcast_dynamic-update-slice_fusion, s32[1024]{0:T(1024)S(1)} %pad_clamp_fusion), kind=kCustom, calls=%fused_computation | custom fusion | bytes 2097184 | tf_op jit(solution)/shard_map/gather | solution.py:54
  40.8 1.9 %fusion.34 = (bf16[1,8,8,16,128]{4,3,2,0,1:T(8,128)(2,1)}, bf16[1,8,8,16,128]{4,3,2,0,1:T(8,128)(2,1)}) fusion(bf16[4,8,8,16,128]{4,3,2,0,1:T(8,128)(2,1)} %bitcast.61), kind=kLoop, calls=%fused_computation.55 | loop fusion | bytes 1048576 | tf_op jit(solution)/shard_map/slice | solution.py:24
  42.7 3.3 %collective-permute-start.7 = (bf16[1,64,16,128]{3,2,1,0:T(8,128)(2,1)}, bf16[1,64,16,128]{3,2,1,0:T(8,128)(2,1)}, u32[]{:S(2)}, u32[]{:S(2)}) collective-permute-start(bf16[1,64,16,128]{3,2,1,0:T(8,128)(2,1)} %bitcast.17), channel_id=1, source_target_pairs={{0,2},{2,4},{4,6},{6,8},{8,10},{10,12},{12,14},{1,3},{3,5},{5,7},{... | collective-permute-start | bytes 786440 | tf_op jit(solution)/shard_map/ppermute | solution.py:26
  46.0 1.3 collective-permute-start.8
  47.3 1.4 copy.14
  48.7 0.8 collective-permute-done.7
  49.5 7.7 %collective-permute-done.8 = bf16[1,64,16,128]{3,2,1,0:T(8,128)(2,1)} collective-permute-done((bf16[1,64,16,128]{3,2,1,0:T(8,128)(2,1)}, bf16[1,64,16,128]{3,2,1,0:T(8,128)(2,1)}, u32[]{:S(2)}, u32[]{:S(2)}) %collective-permute-start.8) | collective-permute-done | bytes 262176 | tf_op jit(solution)/shard_map/ppermute | solution.py:27
  57.2 1.2 maximum_bitcast_fusion
  59.2 1.5 copy.17
  61.4 13.5 %broadcast_select_fusion.1 = f32[4,64,8,3,256]{4,2,3,1,0:T(8,128)S(1)} fusion(pred[8,3]{0,1:T(4,128)(4,1)S(1)} %copy-done.5, bf16[6,64,1,7,2,128]{5,3,4,1,0,2:T(8,128)(2,1)S(1)} %slice.32, bf16[6,64,1,8,3,128]{5,3,4,1,0,2:T(8,128)(2,1)S(1)} %copy.17, bf16[3,3,3,256,256]{4,3,2,1,0:T(8,128)(2,1)S(1)} %copy-done, s32[]{:T(128)S(6)} %select_n.49), kind=kOutput, calls=%fused_computation.19 | convolution fusion | flops 10771759104 | bytes 11993604 | tf_op jit(solution)/shard_map/conv_general_dilated | solution.py:33
  74.9 1.9 %copy.18 = f32[4,64,8,3,256]{4,1,3,2,0:T(8,128)S(1)} copy(f32[4,64,8,3,256]{4,2,3,1,0:T(8,128)S(1)} %broadcast_select_fusion.1) | data formatting | bytes 12582912 | tf_op jit(solution)/shard_map/conv_general_dilated | solution.py:33
  76.8 2.4 %slice_bitcast_fusion.1 = f32[4,64,16,256]{3,1,2,0:T(8,128)} fusion(f32[4,64,1,24,256]{4,1,3,0,2:T(8,128)S(1)} %bitcast.57), kind=kLoop, calls=%fused_computation.5 | loop fusion | bytes 8388608 | tf_op jit(solution)/shard_map/squeeze | solution.py:33
  80.0 14.6 %reduce-scatter.3.cloned.1.call-done = f32[4,64,16,128]{3,1,2,0:T(8,128)} async-done(((f32[4,64,16,256]{3,1,2,0:T(8,128)}), f32[4,64,16,128]{3,1,2,0:T(8,128)}) %reduce-scatter.3.cloned.1.call-update) | async-done | bytes 2097168 | tf_op jit(solution)/shard_map/reduce_scatter | solution.py:61
  94.6 1.9 %maximum_convert_fusion.1 = bf16[4,64,16,128]{3,1,2,0:T(8,128)(2,1)S(1)} fusion(f32[4,64,16,128]{3,1,2,0:T(8,128)} %reduce-scatter.3.cloned.1.call-done, f32[128]{0:T(128)S(1)} %dynamic_slice.45), kind=kLoop, calls=%fused_computation.21 | loop fusion | flops 1572864 | bytes 3146240 | tf_op jit(solution)/shard_map/convert_element_type | solution.py:66
  96.5 1.3 collective-permute-start.10
  97.8 4.7 %collective-permute-start.9 = (bf16[1,64,16,128]{3,1,2,0:T(8,128)(2,1)S(1)}, bf16[1,64,16,128]{3,1,2,0:T(8,128)(2,1)S(1)}, u32[]{:S(2)}, u32[]{:S(2)}) collective-permute-start(bf16[1,64,16,128]{3,1,2,0:T(8,128)(2,1)S(1)} %get-tuple-element.5), channel_id=1, source_target_pairs={{0,2},{2,4},{4,6},{6,8},{8,10},{10,12},{12,14},{1,3},{3,5},{5,7},{... | collective-permute-start | bytes 786440 | tf_op jit(solution)/shard_map/ppermute | solution.py:26
  102.6 4.4 %collective-permute-done.10 = bf16[1,64,16,128]{3,1,2,0:T(8,128)(2,1)S(1)} collective-permute-done((bf16[1,64,16,128]{3,1,2,0:T(8,128)(2,1)S(1)}, bf16[1,64,16,128]{3,1,2,0:T(8,128)(2,1)S(1)}, u32[]{:S(2)}, u32[]{:S(2)}) %collective-permute-start.10) | collective-permute-done | bytes 262176 | tf_op jit(solution)/shard_map/ppermute | solution.py:27
  107.0 5.7 %collective-permute-done.9 = bf16[1,64,16,128]{3,1,2,0:T(8,128)(2,1)S(1)} collective-permute-done((bf16[1,64,16,128]{3,1,2,0:T(8,128)(2,1)S(1)}, bf16[1,64,16,128]{3,1,2,0:T(8,128)(2,1)S(1)}, u32[]{:S(2)}, u32[]{:S(2)}) %collective-permute-start.9) | collective-permute-done | bytes 262176 | tf_op jit(solution)/shard_map/ppermute | solution.py:26
  113.3 1.5 copy.20
  115.3 13.5 %broadcast_select_fusion = f32[4,64,8,3,256]{4,2,3,1,0:T(8,128)S(1)} fusion(pred[8,3]{0,1:T(4,128)(4,1)S(1)} %copy-done.5, bf16[6,64,1,7,2,128]{5,3,4,1,0,2:T(8,128)(2,1)S(1)} %slice.36, bf16[6,64,1,8,3,128]{5,3,4,1,0,2:T(8,128)(2,1)S(1)} %copy.20, bf16[3,3,3,256,256]{4,3,2,1,0:T(8,128)(2,1)S(1)} %copy-done.2, s32[]{:T(128)S(6)} %select_n.49), kind=kOutput, calls=%fused_computation.18 | convolution fusion | flops 10771759104 | bytes 11993604 | tf_op jit(solution)/shard_map/conv_general_dilated | solution.py:33
  128.8 1.9 %copy.21 = f32[4,64,8,3,256]{4,1,3,2,0:T(8,128)S(1)} copy(f32[4,64,8,3,256]{4,2,3,1,0:T(8,128)S(1)} %broadcast_select_fusion) | data formatting | bytes 12582912 | tf_op jit(solution)/shard_map/conv_general_dilated | solution.py:33
  130.7 2.4 %slice_bitcast_fusion = f32[4,64,16,256]{3,1,2,0:T(8,128)} fusion(f32[4,64,1,24,256]{4,1,3,0,2:T(8,128)S(1)} %bitcast.58), kind=kLoop, calls=%fused_computation.4 | loop fusion | bytes 8388608 | tf_op jit(solution)/shard_map/squeeze | solution.py:33
  133.9 12.5 %reduce-scatter.5.cloned.1.call-done = f32[4,64,16,128]{3,1,2,0:T(8,128)} async-done(((f32[4,64,16,256]{3,1,2,0:T(8,128)}), f32[4,64,16,128]{3,1,2,0:T(8,128)}) %reduce-scatter.5.cloned.1.call-update) | async-done | bytes 2097168 | tf_op jit(solution)/shard_map/reduce_scatter | solution.py:61
  146.4 1.9 %maximum_convert_fusion = bf16[4,64,16,128]{3,1,2,0:T(8,128)(2,1)S(1)} fusion(f32[4,64,16,128]{3,1,2,0:T(8,128)} %reduce-scatter.5.cloned.1.call-done, f32[128]{0:T(128)S(1)} %dynamic_slice.47), kind=kLoop, calls=%fused_computation.20 | loop fusion | flops 1572864 | bytes 3146240 | tf_op jit(solution)/shard_map/convert_element_type | solution.py:70
  148.3 1.7 %copy.22 = bf16[4,64,16,128]{3,2,1,0:T(8,128)(2,1)} copy(bf16[4,64,16,128]{3,1,2,0:T(8,128)(2,1)S(1)} %maximum_convert_fusion) | data formatting | bytes 2097152 | tf_op jit(solution)/shard_map/convert_element_type | solution.py:70
  (42 shorter events, 9.8 us)
Async XLA Ops:
  6.5 54.6 %copy-start = (bf16[3,3,3,256,256]{4,3,2,1,0:T(8,128)(2,1)S(1)}, bf16[3,3,3,256,256]{4,3,2,1,0:T(8,128)(2,1)}, u32[]{:S(2)}) copy-start(bf16[3,3,3,256,256]{4,3,2,1,0:T(8,128)(2,1)} %param.6) | copy-start | bytes 10616836
  6.5 88.1 %reduce-scatter.3.cloned.1.call-start = ((), (), s32[]{:S(2)}) async-start(), calls=%async_computation.2 | async-start | bytes 6291456 | tf_op jit(solution)/shard_map/reduce_scatter | solution.py:61
  8.9 8.8 %collective-permute-start = (bf16[4,8,16,128]{3,2,1,0:T(8,128)(2,1)S(1)}, bf16[4,8,16,128]{3,2,1,0:T(8,128)(2,1)S(1)}, u32[]{:S(2)}, u32[]{:S(2)}) collective-permute-start(bf16[4,8,16,128]{3,2,1,0:T(8,128)(2,1)S(1)} %get-tuple-element.15), channel_id=1, source_target_pairs={{0,2},{2,0},{4,6},{6,4},{8,10},{10,8},{12,14},{14,12},{1,3},{3,1},... | collective-permute-start | bytes 393224 | tf_op jit(solution)/shard_map/ppermute | solution.py:53
  11.9 10.7 %collective-permute-start.1 = (bf16[4,8,16,128]{3,2,1,0:T(8,128)(2,1)S(1)}, bf16[4,8,16,128]{3,2,1,0:T(8,128)(2,1)S(1)}, u32[]{:S(2)}, u32[]{:S(2)}) collective-permute-start(bf16[4,8,16,128]{3,2,1,0:T(8,128)(2,1)S(1)} %get-tuple-element.14), channel_id=1, source_target_pairs={{0,4},{2,6},{4,0},{6,2},{8,12},{10,14},{12,8},{14,10},{1,5},{3,7},... | collective-permute-start | bytes 393224 | tf_op jit(solution)/shard_map/ppermute | solution.py:53
  13.5 10.5 %collective-permute-start.2 = (bf16[4,8,16,128]{3,2,1,0:T(8,128)(2,1)S(1)}, bf16[4,8,16,128]{3,2,1,0:T(8,128)(2,1)S(1)}, u32[]{:S(2)}, u32[]{:S(2)}) collective-permute-start(bf16[4,8,16,128]{3,2,1,0:T(8,128)(2,1)S(1)} %get-tuple-element.13), channel_id=1, source_target_pairs={{0,6},{2,4},{4,2},{6,0},{8,14},{10,12},{12,10},{14,8},{1,7},{3,5},... | collective-permute-start | bytes 393224 | tf_op jit(solution)/shard_map/ppermute | solution.py:53
  13.5 11.1 %collective-permute-start.3 = (bf16[4,8,16,128]{3,2,1,0:T(8,128)(2,1)S(1)}, bf16[4,8,16,128]{3,2,1,0:T(8,128)(2,1)S(1)}, u32[]{:S(2)}, u32[]{:S(2)}) collective-permute-start(bf16[4,8,16,128]{3,2,1,0:T(8,128)(2,1)S(1)} %get-tuple-element.12), channel_id=1, source_target_pairs={{0,8},{2,10},{4,12},{6,14},{8,0},{10,2},{12,4},{14,6},{1,9},{3,11}... | collective-permute-start | bytes 393224 | tf_op jit(solution)/shard_map/ppermute | solution.py:53
  16.5 19.5 %collective-permute-start.4 = (bf16[4,8,16,128]{3,2,1,0:T(8,128)(2,1)S(1)}, bf16[4,8,16,128]{3,2,1,0:T(8,128)(2,1)S(1)}, u32[]{:S(2)}, u32[]{:S(2)}) collective-permute-start(bf16[4,8,16,128]{3,2,1,0:T(8,128)(2,1)S(1)} %get-tuple-element.11), channel_id=1, source_target_pairs={{0,10},{2,8},{4,14},{6,12},{8,2},{10,0},{12,6},{14,4},{1,11},{3,9}... | collective-permute-start | bytes 393224 | tf_op jit(solution)/shard_map/ppermute | solution.py:53
  17.8 18.8 %collective-permute-start.5 = (bf16[4,8,16,128]{3,2,1,0:T(8,128)(2,1)S(1)}, bf16[4,8,16,128]{3,2,1,0:T(8,128)(2,1)S(1)}, u32[]{:S(2)}, u32[]{:S(2)}) collective-permute-start(bf16[4,8,16,128]{3,2,1,0:T(8,128)(2,1)S(1)} %get-tuple-element.10), channel_id=1, source_target_pairs={{0,12},{2,14},{4,8},{6,10},{8,4},{10,6},{12,0},{14,2},{1,13},{3,15... | collective-permute-start | bytes 393224 | tf_op jit(solution)/shard_map/ppermute | solution.py:53
  22.6 14.6 %collective-permute-start.6 = (bf16[4,8,16,128]{3,2,1,0:T(8,128)(2,1)S(1)}, bf16[4,8,16,128]{3,2,1,0:T(8,128)(2,1)S(1)}, u32[]{:S(2)}, u32[]{:S(2)}) collective-permute-start(bf16[4,8,16,128]{3,2,1,0:T(8,128)(2,1)S(1)} %get-tuple-element.9), channel_id=1, source_target_pairs={{0,14},{2,12},{4,10},{6,8},{8,6},{10,4},{12,2},{14,0},{1,15},{3,13... | collective-permute-start | bytes 393224 | tf_op jit(solution)/shard_map/ppermute | solution.py:53
  42.7 6.8 %collective-permute-start.7 = (bf16[1,64,16,128]{3,2,1,0:T(8,128)(2,1)}, bf16[1,64,16,128]{3,2,1,0:T(8,128)(2,1)}, u32[]{:S(2)}, u32[]{:S(2)}) collective-permute-start(bf16[1,64,16,128]{3,2,1,0:T(8,128)(2,1)} %bitcast.17), channel_id=1, source_target_pairs={{0,2},{2,4},{4,6},{6,8},{8,10},{10,12},{12,14},{1,3},{3,5},{5,7},{... | collective-permute-start | bytes 786440 | tf_op jit(solution)/shard_map/ppermute | solution.py:26
  46.0 11.2 %collective-permute-start.8 = (bf16[1,64,16,128]{3,2,1,0:T(8,128)(2,1)}, bf16[1,64,16,128]{3,2,1,0:T(8,128)(2,1)}, u32[]{:S(2)}, u32[]{:S(2)}) collective-permute-start(bf16[1,64,16,128]{3,2,1,0:T(8,128)(2,1)} %bitcast.19), channel_id=1, source_target_pairs={{2,0},{4,2},{6,4},{8,6},{10,8},{12,10},{14,12},{3,1},{5,3},{7,5},{... | collective-permute-start | bytes 786440 | tf_op jit(solution)/shard_map/ppermute | solution.py:27
  60.7 0.7 copy-start.5
  79.2 0.7 copy-start.3
  79.3 67.1 %reduce-scatter.5.cloned.1.call-start = ((), (), s32[]{:S(2)}) async-start(), calls=%async_computation.3 | async-start | bytes 6291456 | tf_op jit(solution)/shard_map/reduce_scatter | solution.py:61
  96.5 10.4 %collective-permute-start.10 = (bf16[1,64,16,128]{3,1,2,0:T(8,128)(2,1)S(1)}, bf16[1,64,16,128]{3,1,2,0:T(8,128)(2,1)S(1)}, u32[]{:S(2)}, u32[]{:S(2)}) collective-permute-start(bf16[1,64,16,128]{3,1,2,0:T(8,128)(2,1)S(1)} %get-tuple-element.6), channel_id=1, source_target_pairs={{2,0},{4,2},{6,4},{8,6},{10,8},{12,10},{14,12},{3,1},{5,3},{7,5},{... | collective-permute-start | bytes 786440 | tf_op jit(solution)/shard_map/ppermute | solution.py:27
  97.8 14.9 %collective-permute-start.9 = (bf16[1,64,16,128]{3,1,2,0:T(8,128)(2,1)S(1)}, bf16[1,64,16,128]{3,1,2,0:T(8,128)(2,1)S(1)}, u32[]{:S(2)}, u32[]{:S(2)}) collective-permute-start(bf16[1,64,16,128]{3,1,2,0:T(8,128)(2,1)S(1)} %get-tuple-element.5), channel_id=1, source_target_pairs={{0,2},{2,4},{4,6},{6,8},{8,10},{10,12},{12,14},{1,3},{3,5},{5,7},{... | collective-permute-start | bytes 786440 | tf_op jit(solution)/shard_map/ppermute | solution.py:26
  113.3 2.0 %copy-start.2 = (bf16[3,3,3,256,256]{4,3,2,1,0:T(8,128)(2,1)S(1)}, bf16[3,3,3,256,256]{4,3,2,1,0:T(8,128)(2,1)}, u32[]{:S(2)}) copy-start(bf16[3,3,3,256,256]{4,3,2,1,0:T(8,128)(2,1)} %param.8) | copy-start | bytes 10616836
  133.2 0.7 copy-start.4
  133.8 16.1 %copy-start.1 = (bf16[3,3,3,256,256]{4,3,2,1,0:T(8,128)(2,1)S(1)}, bf16[3,3,3,256,256]{4,3,2,1,0:T(8,128)(2,1)}, u32[]{:S(2)}) copy-start(bf16[3,3,3,256,256]{4,3,2,1,0:T(8,128)(2,1)} %param.6) | copy-start | bytes 10616836
Sparse Core Ops, SparseCore 0:
  79.4 15.1 reduce-scatter.2
  133.3 13.0 reduce-scatter.4
